TPU v7x, 512 devices: a whole 4x4x16 slice. The times are simulated.
512 devices in a mesh: patch: 64 (over x, z_hi, y, core), uly: 8 (over z_lo).
Axes of the slice: x: 4, y: 4, z: 16 (z_hi: 2, z_lo: 8; z = z_hi * 8 + z_lo), core: 2. Of those that a mesh axis runs over, the one named last changes fastest.
Arguments:
- queries: bfloat16 [8192, 3072], P(('patch', 'uly')), may hold values from -512 to 512
- keys_new: bfloat16 [8192, 3072], P(('patch', 'uly')), may hold values from -6 to 6
- values_new: bfloat16 [8192, 3072], P(('patch', 'uly')), may hold values from -6 to 6
- keys_old: bfloat16 [8192, 3072], P(('patch', 'uly')), may hold values from -8 to 8
- values_old: bfloat16 [8192, 3072], P(('patch', 'uly')), may hold values from -6 to 6
- gate_table: float32 [50, 3072], replicated, may hold values from 0.5 to 2
- step_index: int32 [1], replicated, may hold values from 0 to 49
Outputs:
- attended: bfloat16 [8192, 3072], P(('patch', 'uly'))
All inputs are finite; a program needn't handle non-finite values.
Results may differ from a plain program's by a relative error of at most 0.0045.
Values may be sent and summed in bfloat16 or wider, within the bound.
A program may use at most 64 MiB of HBM per device.

v0:
```python
import jax
import jax.numpy as jnp
from jax import lax
from jax.sharding import PartitionSpec as P

HEADS = 24
HEAD_DIM = 128


def sent_together(arrays, axis, dim, along):
    both = jnp.concatenate(arrays, axis=along)
    result, at, outs = (lax.all_gather(both, axis, axis=dim, tiled=True), 0, [])
    for a in arrays:
        outs.append(lax.slice_in_dim(result, at, at + a.shape[along], axis=along))
        at += a.shape[along]
    return tuple(outs)


def absorb(carry, query_heads, key_piece, value_piece, masked):
    run_max, run_total, accumulated = carry
    score = jnp.einsum(
        "phd,khd->hpk", query_heads, key_piece, preferred_element_type=jnp.float32
    ) * HEAD_DIM ** (-0.5)
    score = jnp.where(masked[None, None, :], jnp.float32(-1e30), score)
    new_max = jnp.maximum(run_max, jnp.max(score, axis=-1))
    shrink = jnp.exp(run_max - new_max)
    expo = jnp.exp(score - new_max[..., None])
    run_total = run_total * shrink + jnp.sum(expo, axis=-1)
    update = jnp.einsum(
        "hpk,khd->phd", expo.astype(jnp.bfloat16), value_piece, preferred_element_type=jnp.float32
    )
    accumulated = accumulated * jnp.transpose(shrink)[..., None] + update
    return (new_max, run_total, accumulated)


def absorb_blocks(carry, query_heads, key_piece, value_piece, masked):
    count = key_piece.shape[0]
    span = 2048
    heads_here = key_piece.shape[1]
    key_blocks = key_piece.reshape(count // span, span, heads_here, HEAD_DIM)
    value_blocks = value_piece.reshape(count // span, span, heads_here, HEAD_DIM)
    mask_blocks = masked.reshape(count // span, span)

    def one_block(state, pieces):
        return (absorb(state, query_heads, pieces[0], pieces[1], pieces[2]), None)

    carry, unused = lax.scan(one_block, carry, (key_blocks, value_blocks, mask_blocks))
    return carry


def body(queries, keys_new, values_new, keys_old, values_old, gate_table, step_index):
    groups = lax.axis_size("uly")
    heads_here = HEADS // groups
    width_here = heads_here * HEAD_DIM
    patch_here = lax.axis_index("patch")
    fresh = (
        lax.all_to_all(queries, "uly", split_axis=1, concat_axis=0, tiled=True),
        lax.all_to_all(keys_new, "uly", split_axis=1, concat_axis=0, tiled=True),
        lax.all_to_all(values_new, "uly", split_axis=1, concat_axis=0, tiled=True),
    )
    query_heads = fresh[0].reshape(-1, heads_here, HEAD_DIM)
    fresh_keys = fresh[1].reshape(-1, heads_here, HEAD_DIM)
    fresh_values = fresh[2].reshape(-1, heads_here, HEAD_DIM)
    patch_rows = query_heads.shape[0]
    score = jnp.einsum(
        "phd,khd->hpk", query_heads, fresh_keys, preferred_element_type=jnp.float32
    ) * HEAD_DIM ** (-0.5)
    run_max = jnp.max(score, axis=-1)
    expo = jnp.exp(score - run_max[..., None])
    run_total = jnp.sum(expo, axis=-1)
    accumulated = jnp.einsum(
        "hpk,khd->phd", expo.astype(jnp.bfloat16), fresh_values, preferred_element_type=jnp.float32
    )
    carry = (run_max, run_total, accumulated)
    stale = (
        lax.all_to_all(keys_old, "uly", split_axis=1, concat_axis=0, tiled=True),
        lax.all_to_all(values_old, "uly", split_axis=1, concat_axis=0, tiled=True),
    )
    stale_keys = stale[0].reshape(-1, heads_here, HEAD_DIM)
    stale_values = stale[1].reshape(-1, heads_here, HEAD_DIM)
    pieces = sent_together((stale_keys, stale_values), "patch", 0, 1)
    count = pieces[0].shape[0]
    masked = jnp.arange(count, dtype=jnp.int32) // patch_rows == patch_here
    carry = absorb_blocks(carry, query_heads, pieces[0], pieces[1], masked)
    run_max, run_total, accumulated = carry
    picker = (jnp.arange(gate_table.shape[0], dtype=jnp.int32) == step_index[0]).astype(jnp.float32)
    gate = jnp.dot(picker, gate_table, precision=lax.Precision.HIGHEST)
    gate_here = lax.dynamic_slice_in_dim(gate, lax.axis_index("uly") * width_here, width_here, 0)
    mixed = (accumulated / jnp.transpose(run_total)[..., None]).reshape(patch_rows, width_here)
    gated = (mixed * gate_here).astype(jnp.bfloat16)
    return lax.all_to_all(gated, "uly", split_axis=0, concat_axis=1, tiled=True)


def solution(mesh):
    in_specs = (
        P(("patch", "uly"), None),
        P(("patch", "uly"), None),
        P(("patch", "uly"), None),
        P(("patch", "uly"), None),
        P(("patch", "uly"), None),
        P(),
        P(),
    )
    out_specs = P(("patch", "uly"), None)
    return jax.shard_map(body, mesh=mesh, in_specs=in_specs, out_specs=out_specs, check_vma=False)
```

profile of v0, /device:TPU:8, one launch (start us, length us, event | category | flops | bytes accessed | tf_op | source)
XLA Modules:
  0.0 314.0 jit_solution(12219189061899668328)
XLA Ops:
  6.5 0.0 copy-start
  6.5 1.6 copy.86
  8.1 12.5 %all-to-all-start.3 = ((bf16[16,8,384]{2,0,1:T(8,128)(2,1)}), bf16[16,8,384]{2,0,1:T(8,128)(2,1)S(1)}, u32[]{:S(2)}, u32[]{:S(2)}) async-start(bf16[16,8,384]{2,0,1:T(8,128)(2,1)} %bitcast.72), calls=%async_computation.3 | async-start | bytes 196608 | tf_op jit(solution)/shard_map/all_to_all | solution.py:76
  20.7 1.5 copy.85
  22.2 9.7 %all-to-all-done.3 = bf16[16,8,384]{2,0,1:T(8,128)(2,1)S(1)} async-done(((bf16[16,8,384]{2,0,1:T(8,128)(2,1)}), bf16[16,8,384]{2,0,1:T(8,128)(2,1)S(1)}, u32[]{:S(2)}, u32[]{:S(2)}) %all-to-all-start.3) | async-done | bytes 98336 | tf_op jit(solution)/shard_map/all_to_all | solution.py:76
  31.9 3.6 %all-to-all-start.4 = ((bf16[16,8,384]{2,0,1:T(8,128)(2,1)}), bf16[16,8,384]{2,0,1:T(8,128)(2,1)S(1)}, u32[]{:S(2)}, u32[]{:S(2)}) async-start(bf16[16,8,384]{2,0,1:T(8,128)(2,1)} %bitcast.71), calls=%async_computation.4 | async-start | bytes 196608 | tf_op jit(solution)/shard_map/all_to_all | solution.py:77
  35.5 0.0 all-gather.2.cloned.1.call-start
  35.6 11.1 %all-to-all-done.4 = bf16[16,8,384]{2,0,1:T(8,128)(2,1)S(1)} async-done(((bf16[16,8,384]{2,0,1:T(8,128)(2,1)}), bf16[16,8,384]{2,0,1:T(8,128)(2,1)S(1)}, u32[]{:S(2)}, u32[]{:S(2)}) %all-to-all-start.4) | async-done | bytes 98336 | tf_op jit(solution)/shard_map/all_to_all | solution.py:77
  46.7 0.1 pad_maximum_fusion
  46.9 0.7 copy.57
  47.6 0.0 all-gather.2.cloned.1.call-update
  47.6 1.5 copy.89
  49.2 3.5 %all-to-all-start = ((bf16[16,8,384]{2,0,1:T(8,128)(2,1)}), bf16[16,8,384]{2,0,1:T(8,128)(2,1)S(1)}, u32[]{:S(2)}, u32[]{:S(2)}) async-start(bf16[16,8,384]{2,0,1:T(8,128)(2,1)} %bitcast.75), calls=%async_computation | async-start | bytes 196608 | tf_op jit(solution)/shard_map/all_to_all | solution.py:57
  52.6 1.5 copy.88
  54.2 9.6 %all-to-all-done = bf16[16,8,384]{2,0,1:T(8,128)(2,1)S(1)} async-done(((bf16[16,8,384]{2,0,1:T(8,128)(2,1)}), bf16[16,8,384]{2,0,1:T(8,128)(2,1)S(1)}, u32[]{:S(2)}, u32[]{:S(2)}) %all-to-all-start) | async-done | bytes 98336 | tf_op jit(solution)/shard_map/all_to_all | solution.py:57
  63.8 3.4 %all-to-all-start.1 = ((bf16[16,8,384]{2,0,1:T(8,128)(2,1)}), bf16[16,8,384]{2,0,1:T(8,128)(2,1)S(1)}, u32[]{:S(2)}, u32[]{:S(2)}) async-start(bf16[16,8,384]{2,0,1:T(8,128)(2,1)} %bitcast.74), calls=%async_computation.1 | async-start | bytes 196608 | tf_op jit(solution)/shard_map/all_to_all | solution.py:58
  67.2 0.0 copy-done.1
  67.2 0.7 copy.87
  68.5 13.1 %all-to-all-done.1 = bf16[16,8,384]{2,0,1:T(8,128)(2,1)S(1)} async-done(((bf16[16,8,384]{2,0,1:T(8,128)(2,1)}), bf16[16,8,384]{2,0,1:T(8,128)(2,1)S(1)}, u32[]{:S(2)}, u32[]{:S(2)}) %all-to-all-start.1) | async-done | bytes 98336 | tf_op jit(solution)/shard_map/all_to_all | solution.py:58
  81.6 3.4 %all-to-all-start.2 = ((bf16[16,8,384]{2,0,1:T(8,128)(2,1)}), bf16[16,8,384]{2,0,1:T(8,128)(2,1)S(1)}, u32[]{:S(2)}, u32[]{:S(2)}) async-start(bf16[16,8,384]{2,0,1:T(8,128)(2,1)} %bitcast.73), calls=%async_computation.2 | async-start | bytes 196608 | tf_op jit(solution)/shard_map/all_to_all | solution.py:59
  85.0 0.0 copy-done
  85.0 0.3 fusion.33
  85.3 0.1 dynamic_slice.14
  85.4 0.1 fusion.30
  85.6 10.6 %all-to-all-done.2 = bf16[16,8,384]{2,0,1:T(8,128)(2,1)S(1)} async-done(((bf16[16,8,384]{2,0,1:T(8,128)(2,1)}), bf16[16,8,384]{2,0,1:T(8,128)(2,1)S(1)}, u32[]{:S(2)}, u32[]{:S(2)}) %all-to-all-start.2) | async-done | bytes 98336 | tf_op jit(solution)/shard_map/all_to_all | solution.py:59
  96.2 0.2 fusion.39
  96.5 0.2 convolution_bitcast_fusion
  96.7 0.1 copy.58
  96.8 0.1 fusion.24
  96.9 165.4 %all-gather.2.cloned.1.call-done = bf16[8192,6,128]{2,0,1:T(8,128)(2,1)} async-done(((bf16[128,6,128]{2,0,1:T(8,128)(2,1)}), bf16[8192,6,128]{2,0,1:T(8,128)(2,1)}) %all-gather.2.cloned.1.call-update) | async-done | bytes 12582928 | tf_op jit(solution)/shard_map/all_gather | solution.py:12
  262.3 10.1 %fusion.38 = (bf16[8192,3,128]{2,0,1:T(8,128)(2,1)}, bf16[8192,3,128]{2,0,1:T(8,128)(2,1)}) fusion(bf16[8192,6,128]{2,0,1:T(8,128)(2,1)} %all-gather.2.cloned.1.call-done), kind=kLoop, calls=%fused_computation.51 | loop fusion | bytes 25165824 | tf_op jit(solution)/shard_map/slice | solution.py:14
  272.4 19.6 %while.14 = (s32[]{:T(128)}, f32[3,128]{1,0:T(4,128)S(1)}, f32[3,128]{1,0:T(4,128)S(1)}, f32[128,3,128]{0,2,1:T(8,128)S(1)}, pred[4,2048]{1,0:T(4,128)(4,1)S(1)}...) while((s32[]{:T(128)}, f32[3,128]{1,0:T(4,128)S(1)}, ...), condition=%wide.region_5.6_spmd, body=%wide.region_2.5_spmd.sunk | while | flops 408257664 | bytes 13106273 | solution.py:47
  272.4 2.0 bitcast_reduce_fusion.2
  274.4 2.4 fusion.54
  276.8 0.4 fusion.53
  277.3 2.0 bitcast_reduce_fusion.2
  279.4 2.4 fusion.54
  281.7 0.4 fusion.53
  282.2 2.0 bitcast_reduce_fusion.2
  284.3 2.4 fusion.54
  286.6 0.4 fusion.53
  287.1 2.0 bitcast_reduce_fusion.2
  289.2 2.4 fusion.54
  291.5 0.4 fusion.53
  292.0 0.1 copy.62
  292.2 0.1 reshape.75
  292.3 14.2 %all_to_all.96 = bf16[8,16,384]{2,1,0:T(8,128)(2,1)S(1)} all-to-all(bf16[8,16,384]{2,1,0:T(8,128)(2,1)S(1)} %multiply_convert_fusion), channel_id=1, replica_groups=mesh['patch'=64,'uly'=8] {'uly'}, dimensions={0} | all-to-all | bytes 196608 | tf_op jit(solution)/shard_map/all_to_all | solution.py:91
  306.5 0.7 copy.73
  (25 shorter events, 0.5 us)
Async XLA Ops:
  6.5 78.5 %copy-start = (f32[50,3072]{1,0:T(8,128)S(1)}, f32[50,3072]{1,0:T(8,128)}, u32[]{:S(2)}) copy-start(f32[50,3072]{1,0:T(8,128)} %param.14) | copy-start | bytes 1843204
  6.5 60.7 %copy-start.1 = (bf16[16,3072]{1,0:T(8,128)(2,1)S(1)}, bf16[16,3072]{1,0:T(8,128)(2,1)}, u32[]{:S(2)}) copy-start(bf16[16,3072]{1,0:T(8,128)(2,1)} %param.11) | copy-start | bytes 294916
  8.1 23.8 %all-to-all-start.3 = ((bf16[16,8,384]{2,0,1:T(8,128)(2,1)}), bf16[16,8,384]{2,0,1:T(8,128)(2,1)S(1)}, u32[]{:S(2)}, u32[]{:S(2)}) async-start(bf16[16,8,384]{2,0,1:T(8,128)(2,1)} %bitcast.72), calls=%async_computation.3 | async-start | bytes 196608 | tf_op jit(solution)/shard_map/all_to_all | solution.py:76
  31.9 14.8 %all-to-all-start.4 = ((bf16[16,8,384]{2,0,1:T(8,128)(2,1)}), bf16[16,8,384]{2,0,1:T(8,128)(2,1)S(1)}, u32[]{:S(2)}, u32[]{:S(2)}) async-start(bf16[16,8,384]{2,0,1:T(8,128)(2,1)} %bitcast.71), calls=%async_computation.4 | async-start | bytes 196608 | tf_op jit(solution)/shard_map/all_to_all | solution.py:77
  35.5 226.8 %all-gather.2.cloned.1.call-start = ((), (), s32[]{:S(2)}) async-start(), calls=%async_computation.6 | async-start | bytes 12779520 | tf_op jit(solution)/shard_map/all_gather | solution.py:12
  49.2 14.6 %all-to-all-start = ((bf16[16,8,384]{2,0,1:T(8,128)(2,1)}), bf16[16,8,384]{2,0,1:T(8,128)(2,1)S(1)}, u32[]{:S(2)}, u32[]{:S(2)}) async-start(bf16[16,8,384]{2,0,1:T(8,128)(2,1)} %bitcast.75), calls=%async_computation | async-start | bytes 196608 | tf_op jit(solution)/shard_map/all_to_all | solution.py:57
  63.8 17.8 %all-to-all-start.1 = ((bf16[16,8,384]{2,0,1:T(8,128)(2,1)}), bf16[16,8,384]{2,0,1:T(8,128)(2,1)S(1)}, u32[]{:S(2)}, u32[]{:S(2)}) async-start(bf16[16,8,384]{2,0,1:T(8,128)(2,1)} %bitcast.74), calls=%async_computation.1 | async-start | bytes 196608 | tf_op jit(solution)/shard_map/all_to_all | solution.py:58
  81.6 14.6 %all-to-all-start.2 = ((bf16[16,8,384]{2,0,1:T(8,128)(2,1)}), bf16[16,8,384]{2,0,1:T(8,128)(2,1)S(1)}, u32[]{:S(2)}, u32[]{:S(2)}) async-start(bf16[16,8,384]{2,0,1:T(8,128)(2,1)} %bitcast.73), calls=%async_computation.2 | async-start | bytes 196608 | tf_op jit(solution)/shard_map/all_to_all | solution.py:59
Sparse Core Ops, SparseCore 0:
  47.7 214.5 all-gather.1
where the time goes:
time: 315 us; the launch traced here: 314 us
  waiting for transfers between devices  220 us (70%)
  starting transfers between devices  26.4 us (8%)
  local copies, waits for them, and re-layouts  19.1 us (6%)
  matrix products  18.3 us (6%)
  blocking collectives  14.2 us (5%)
  between operations  14.2 us (5%)
    all_gather x1, waiting for transfers between devices, sent_together(): result, at, outs = (lax.all_gather(both, axis, axis=dim, tiled=True), 0, [])  165 us
    all_to_all x1, blocking collectives, body(): return lax.all_to_all(gated, 'uly', split_axis=0, concat_axis=1, tiled=True)  14.2 us
    all_to_all x1, waiting for transfers between devices, body(): lax.all_to_all(keys_new, 'uly', split_axis=1, concat_axis=0, tiled=True)  13.1 us
    all_to_all x1, starting transfers between devices, body(): lax.all_to_all(keys_old, 'uly', split_axis=1, concat_axis=0, tiled=True)  12.5 us
    all_to_all x1, waiting for transfers between devices, body(): lax.all_to_all(values_old, 'uly', split_axis=1, concat_axis=0, tiled=True)  11.1 us
    all_to_all x1, waiting for transfers between devices, body(): lax.all_to_all(values_new, 'uly', split_axis=1, concat_axis=0, tiled=True)  10.6 us
    slice x1, local copies, waits for them, and re-layouts, sent_together(): outs.append(lax.slice_in_dim(result, at, at + a.shape[along], axis=along))  10.1 us
    all_to_all x1, waiting for transfers between devices, body(): lax.all_to_all(keys_old, 'uly', split_axis=1, concat_axis=0, tiled=True)  9.72 us
  transfers between devices with their start and end apart: 6, of which 6 were waited for; matrix products, arithmetic and copies ran while one was open for 2% of the time, Pallas kernels for 0%

commit v1 on v0

--- a/solution.py
+++ b/solution.py
@@ -74,7 +74,12 @@
     carry = (run_max, run_total, accumulated)
     stale = (
         lax.all_to_all(keys_old, "uly", split_axis=1, concat_axis=0, tiled=True),
-        lax.all_to_all(values_old, "uly", split_axis=1, concat_axis=0, tiled=True),
+        jnp.concatenate(
+            lax.all_to_all(
+                jnp.stack(jnp.split(values_old, lax.axis_size("uly"), axis=1)), "uly", 0, 0
+            ),
+            axis=0,
+        ),
     )
     stale_keys = stale[0].reshape(-1, heads_here, HEAD_DIM)
     stale_values = stale[1].reshape(-1, heads_here, HEAD_DIM)

time: 315 us -> 322 us (1.022)
  local copies, waits for them, and re-layouts: 19.1 us -> 28.1 us
  waiting for transfers between devices: 220 us -> 212 us
  starting transfers between devices: 26.4 us -> 32 us
    unnamed x4 -> x11, local copies, waits for them, and re-layouts: 0.01 us -> 9.16 us
    all_to_all x1, waiting for transfers between devices: 9.72 us -> 0.8 us  [body(): lax.all_to_all(keys_old, 'uly', split_axis=1, concat_axis=0, tiled=True)]
    all_to_all x1, starting transfers between devices: 3.6 us -> 9.11 us  [body(): lax.all_to_all(jnp.stack(jnp.split(values_old, lax.axis_size('uly'), axis...]
  transfers between devices with their start and end apart: 6 -> 6, of which waited for: 6 -> 6; matrix products, arithmetic and copies ran while one was open for 2% -> 5% of each run, Pallas kernels for 0% -> 0%
where the time goes in v1:
time: 322 us; the launch traced here: 321 us
  waiting for transfers between devices  212 us (66%)
  starting transfers between devices  32 us (10%)
  local copies, waits for them, and re-layouts  28.1 us (9%)
  matrix products  18.3 us (6%)
  blocking collectives  14.2 us (4%)
  between operations  14.2 us (4%)
    all_gather x1, waiting for transfers between devices, sent_together(): result, at, outs = (lax.all_gather(both, axis, axis=dim, tiled=True), 0, [])  168 us
    all_to_all x1, blocking collectives, body(): return lax.all_to_all(gated, 'uly', split_axis=0, concat_axis=1, tiled=True)  14.2 us
    all_to_all x1, starting transfers between devices, body(): lax.all_to_all(keys_old, 'uly', split_axis=1, concat_axis=0, tiled=True)  12.5 us
    all_to_all x1, waiting for transfers between devices, body(): lax.all_to_all(keys_new, 'uly', split_axis=1, concat_axis=0, tiled=True)  12 us
    all_to_all x1, waiting for transfers between devices, body(): lax.all_to_all(jnp.stack(jnp.split(values_old, lax.axis_size('uly'), axis...  11.1 us
    all_to_all x1, waiting for transfers between devices, body(): lax.all_to_all(values_new, 'uly', split_axis=1, concat_axis=0, tiled=True)  10.6 us
    slice x1, local copies, waits for them, and re-layouts, sent_together(): outs.append(lax.slice_in_dim(result, at, at + a.shape[along], axis=along))  10.1 us
    all_to_all x1, waiting for transfers between devices, body(): lax.all_to_all(queries, 'uly', split_axis=1, concat_axis=0, tiled=True)  9.56 us
  transfers between devices with their start and end apart: 6, of which 6 were waited for; matrix products, arithmetic and copies ran while one was open for 5% of the time, Pallas kernels for 0%

profile of v1, /device:TPU:8, one launch (start us, length us, event | category | flops | bytes accessed | tf_op | source)
XLA Modules:
  0.0 320.9 jit_solution(7305848134880846)
XLA Ops:
  6.5 1.6 copy.81
  8.1 12.5 %all-to-all-start.3 = ((bf16[16,8,384]{2,0,1:T(8,128)(2,1)}), bf16[16,8,384]{2,0,1:T(8,128)(2,1)S(1)}, u32[]{:S(2)}, u32[]{:S(2)}) async-start(bf16[16,8,384]{2,0,1:T(8,128)(2,1)} %bitcast.83), calls=%async_computation.3 | async-start | bytes 196608 | tf_op jit(solution)/shard_map/all_to_all | solution.py:76
  20.7 1.3 constant_dynamic-update-slice_fusion.7
  22.0 1.3 constant_dynamic-update-slice_fusion.6
  23.3 1.3 constant_dynamic-update-slice_fusion.5
  24.6 1.3 constant_dynamic-update-slice_fusion.4
  25.9 1.3 constant_dynamic-update-slice_fusion.3
  27.2 1.3 constant_dynamic-update-slice_fusion.2
  28.5 1.3 constant_dynamic-update-slice_fusion.1
  29.8 1.3 constant_dynamic-update-slice_fusion
  31.1 0.8 all-to-all-done.3
  31.9 9.1 %all-to-all-start.4 = ((bf16[8,16,384]{2,1,0:T(8,128)(2,1)}), bf16[8,16,384]{2,1,0:T(8,128)(2,1)S(1)}, u32[]{:S(2)}, u32[]{:S(2)}) async-start(bf16[8,16,384]{2,1,0:T(8,128)(2,1)} %constant_dynamic-update-slice_fusion), calls=%async_computation.4 | async-start | bytes 196608 | tf_op jit(solution)/shard_map/all_to_all | solution.py:78
  41.1 11.1 %all-to-all-done.4 = bf16[8,16,384]{2,1,0:T(8,128)(2,1)S(1)} async-done(((bf16[8,16,384]{2,1,0:T(8,128)(2,1)}), bf16[8,16,384]{2,1,0:T(8,128)(2,1)S(1)}, u32[]{:S(2)}, u32[]{:S(2)}) %all-to-all-start.4) | async-done | bytes 98336 | tf_op jit(solution)/shard_map/all_to_all | solution.py:78
  52.2 0.1 pad_maximum_fusion
  52.4 0.7 copy.55
  53.1 1.5 copy.84
  54.7 3.4 %all-to-all-start = ((bf16[16,8,384]{2,0,1:T(8,128)(2,1)}), bf16[16,8,384]{2,0,1:T(8,128)(2,1)S(1)}, u32[]{:S(2)}, u32[]{:S(2)}) async-start(bf16[16,8,384]{2,0,1:T(8,128)(2,1)} %bitcast.86), calls=%async_computation | async-start | bytes 196608 | tf_op jit(solution)/shard_map/all_to_all | solution.py:57
  58.0 1.5 copy.83
  59.6 9.6 %all-to-all-done = bf16[16,8,384]{2,0,1:T(8,128)(2,1)S(1)} async-done(((bf16[16,8,384]{2,0,1:T(8,128)(2,1)}), bf16[16,8,384]{2,0,1:T(8,128)(2,1)S(1)}, u32[]{:S(2)}, u32[]{:S(2)}) %all-to-all-start) | async-done | bytes 98336 | tf_op jit(solution)/shard_map/all_to_all | solution.py:57
  69.1 3.4 %all-to-all-start.1 = ((bf16[16,8,384]{2,0,1:T(8,128)(2,1)}), bf16[16,8,384]{2,0,1:T(8,128)(2,1)S(1)}, u32[]{:S(2)}, u32[]{:S(2)}) async-start(bf16[16,8,384]{2,0,1:T(8,128)(2,1)} %bitcast.85), calls=%async_computation.1 | async-start | bytes 196608 | tf_op jit(solution)/shard_map/all_to_all | solution.py:58
  72.5 0.7 copy.82
  73.8 12.0 %all-to-all-done.1 = bf16[16,8,384]{2,0,1:T(8,128)(2,1)S(1)} async-done(((bf16[16,8,384]{2,0,1:T(8,128)(2,1)}), bf16[16,8,384]{2,0,1:T(8,128)(2,1)S(1)}, u32[]{:S(2)}, u32[]{:S(2)}) %all-to-all-start.1) | async-done | bytes 98336 | tf_op jit(solution)/shard_map/all_to_all | solution.py:58
  85.8 3.6 %all-to-all-start.2 = ((bf16[16,8,384]{2,0,1:T(8,128)(2,1)}), bf16[16,8,384]{2,0,1:T(8,128)(2,1)S(1)}, u32[]{:S(2)}, u32[]{:S(2)}) async-start(bf16[16,8,384]{2,0,1:T(8,128)(2,1)} %bitcast.84), calls=%async_computation.2 | async-start | bytes 196608 | tf_op jit(solution)/shard_map/all_to_all | solution.py:59
  89.4 0.3 fusion.33
  89.8 0.1 dynamic_slice.14
  90.0 10.6 %all-to-all-done.2 = bf16[16,8,384]{2,0,1:T(8,128)(2,1)S(1)} async-done(((bf16[16,8,384]{2,0,1:T(8,128)(2,1)}), bf16[16,8,384]{2,0,1:T(8,128)(2,1)S(1)}, u32[]{:S(2)}, u32[]{:S(2)}) %all-to-all-start.2) | async-done | bytes 98336 | tf_op jit(solution)/shard_map/all_to_all | solution.py:59
  100.6 0.2 fusion.39
  100.8 0.2 convolution_bitcast_fusion
  101.1 0.1 copy.56
  101.3 167.9 %all-gather.2.cloned.1.call-done = bf16[8192,6,128]{2,0,1:T(8,128)(2,1)} async-done(((bf16[128,6,128]{2,0,1:T(8,128)(2,1)}), bf16[8192,6,128]{2,0,1:T(8,128)(2,1)}) %all-gather.2.cloned.1.call-update) | async-done | bytes 12582928 | tf_op jit(solution)/shard_map/all_gather | solution.py:12
  269.2 10.1 %fusion.38 = (bf16[8192,3,128]{2,0,1:T(8,128)(2,1)}, bf16[8192,3,128]{2,0,1:T(8,128)(2,1)}) fusion(bf16[8192,6,128]{2,0,1:T(8,128)(2,1)} %all-gather.2.cloned.1.call-done), kind=kLoop, calls=%fused_computation.58 | loop fusion | bytes 25165824 | tf_op jit(solution)/shard_map/slice | solution.py:14
  279.3 19.6 %while.14 = (s32[]{:T(128)}, f32[3,128]{1,0:T(4,128)S(1)}, f32[3,128]{1,0:T(4,128)S(1)}, f32[128,3,128]{0,2,1:T(8,128)S(1)}, pred[4,2048]{1,0:T(4,128)(4,1)S(1)}...) while((s32[]{:T(128)}, f32[3,128]{1,0:T(4,128)S(1)}, ...), condition=%wide.region_5.6_spmd, body=%wide.region_2.5_spmd.sunk | while | flops 408257664 | bytes 13106273 | solution.py:47
  279.3 2.0 bitcast_reduce_fusion.2
  281.3 2.4 fusion.54
  283.7 0.4 fusion.53
  284.2 2.0 bitcast_reduce_fusion.2
  286.2 2.4 fusion.54
  288.6 0.4 fusion.53
  289.1 2.0 bitcast_reduce_fusion.2
  291.2 2.4 fusion.54
  293.5 0.4 fusion.53
  294.0 2.0 bitcast_reduce_fusion.2
  296.1 2.4 fusion.54
  298.4 0.4 fusion.53
  298.9 0.1 copy.60
  299.1 0.1 reshape.67
  299.2 14.2 %all_to_all.85 = bf16[8,16,384]{2,1,0:T(8,128)(2,1)S(1)} all-to-all(bf16[8,16,384]{2,1,0:T(8,128)(2,1)S(1)} %multiply_convert_fusion), channel_id=1, replica_groups=mesh['patch'=64,'uly'=8] {'uly'}, dimensions={0} | all-to-all | bytes 196608 | tf_op jit(solution)/shard_map/all_to_all | solution.py:96
  313.4 0.7 copy.70
  (32 shorter events, 0.7 us)
Async XLA Ops:
  6.5 82.9 %copy-start = (f32[50,3072]{1,0:T(8,128)S(1)}, f32[50,3072]{1,0:T(8,128)}, u32[]{:S(2)}) copy-start(f32[50,3072]{1,0:T(8,128)} %param.14) | copy-start | bytes 1843204
  6.5 66.0 %copy-start.1 = (bf16[16,3072]{1,0:T(8,128)(2,1)S(1)}, bf16[16,3072]{1,0:T(8,128)(2,1)}, u32[]{:S(2)}) copy-start(bf16[16,3072]{1,0:T(8,128)(2,1)} %param.11) | copy-start | bytes 294916
  8.1 23.8 %all-to-all-start.3 = ((bf16[16,8,384]{2,0,1:T(8,128)(2,1)}), bf16[16,8,384]{2,0,1:T(8,128)(2,1)S(1)}, u32[]{:S(2)}, u32[]{:S(2)}) async-start(bf16[16,8,384]{2,0,1:T(8,128)(2,1)} %bitcast.83), calls=%async_computation.3 | async-start | bytes 196608 | tf_op jit(solution)/shard_map/all_to_all | solution.py:76
  31.9 20.3 %all-to-all-start.4 = ((bf16[8,16,384]{2,1,0:T(8,128)(2,1)}), bf16[8,16,384]{2,1,0:T(8,128)(2,1)S(1)}, u32[]{:S(2)}, u32[]{:S(2)}) async-start(bf16[8,16,384]{2,1,0:T(8,128)(2,1)} %constant_dynamic-update-slice_fusion), calls=%async_computation.4 | async-start | bytes 196608 | tf_op jit(solution)/shard_map/all_to_all | solution.py:78
  41.0 228.1 %all-gather.2.cloned.1.call-start = ((), (), s32[]{:S(2)}) async-start(), calls=%async_computation.6 | async-start | bytes 12779520 | tf_op jit(solution)/shard_map/all_gather | solution.py:12
  54.7 14.5 %all-to-all-start = ((bf16[16,8,384]{2,0,1:T(8,128)(2,1)}), bf16[16,8,384]{2,0,1:T(8,128)(2,1)S(1)}, u32[]{:S(2)}, u32[]{:S(2)}) async-start(bf16[16,8,384]{2,0,1:T(8,128)(2,1)} %bitcast.86), calls=%async_computation | async-start | bytes 196608 | tf_op jit(solution)/shard_map/all_to_all | solution.py:57
  69.1 16.7 %all-to-all-start.1 = ((bf16[16,8,384]{2,0,1:T(8,128)(2,1)}), bf16[16,8,384]{2,0,1:T(8,128)(2,1)S(1)}, u32[]{:S(2)}, u32[]{:S(2)}) async-start(bf16[16,8,384]{2,0,1:T(8,128)(2,1)} %bitcast.85), calls=%async_computation.1 | async-start | bytes 196608 | tf_op jit(solution)/shard_map/all_to_all | solution.py:58
  85.8 14.8 %all-to-all-start.2 = ((bf16[16,8,384]{2,0,1:T(8,128)(2,1)}), bf16[16,8,384]{2,0,1:T(8,128)(2,1)S(1)}, u32[]{:S(2)}, u32[]{:S(2)}) async-start(bf16[16,8,384]{2,0,1:T(8,128)(2,1)} %bitcast.84), calls=%async_computation.2 | async-start | bytes 196608 | tf_op jit(solution)/shard_map/all_to_all | solution.py:59
Sparse Core Ops, SparseCore 0:
  53.2 215.8 all-gather.1
